TPU v7x, 32 devices: a whole 2x2x4 slice. The times are simulated.
32 devices in a mesh: lat: 4 (over y, core), lon: 8 (over z, x).
Axes of the slice: x: 2, y: 2, z: 4, core: 2. Of those that a mesh axis runs over, the one named last changes fastest.
Arguments:
- field: bfloat16 [64, 128, 384], P('lat', 'lon'), may hold values from -6 to 6
- obs_jac: bfloat16 [32, 32, 128, 384], P(None, ('lat', 'lon')), may hold values from -0.3125 to 0.3125
- obs_frac: bfloat16 [32, 32, 2, 128], P(None, ('lat', 'lon')), may hold values from 0 to 1
- obs_innov: bfloat16 [32, 32, 128], P(None, ('lat', 'lon')), may hold values from -6 to 6
- obs_rinv: bfloat16 [32, 32, 128], P(None, ('lat', 'lon')), may hold values from 1 to 16
- obs_cells: int32 [32, 32, 128], P(None, ('lat', 'lon')), may hold values from -1 to 270, as said below
Outputs:
- departures: float32 [32, 32, 128], P(None, ('lat', 'lon'))
- field_grad: float32 [64, 128, 384], P('lat', 'lon')
Inputs may be any that keep to these rules, and one draw needn't show every extreme that they name: `obs_cells`: in block (o, p) the live slots come first, at least one and at most 128; a live slot holds r * 17 + q with r below 16 and q below 16; slot 0 of every block holds the cell at r = 15, q = 15; the number of live slots varies by owner.
All inputs are finite; a program needn't handle non-finite values.
Results may differ from a plain program's by a relative error of at most 0.0046.
Values may be sent and summed in bfloat16 or wider, within the bound.
A program may use at most 128 MiB of HBM per device.

v0:
```python
import jax
import jax.numpy as jnp
from jax import lax
from jax.sharding import PartitionSpec as P


def shifted(block, axis, distance):
    devices = range(lax.axis_size(axis))
    route = [(i - distance, i) for i in devices if i - distance in devices]
    return lax.ppermute(block, axis, route)


def passed_along(value, axis, steps):
    count = lax.axis_size(axis)
    pairs = [(source, (source + steps) % count) for source in range(count)]
    return lax.ppermute(value, axis, pairs)


def bilinear_weights(frac_lat, frac_lon):
    lat_part = frac_lat.astype(jnp.float32)
    lon_part = frac_lon.astype(jnp.float32)
    raw_weights = (
        (1.0 - lat_part) * (1.0 - lon_part),
        lat_part * (1.0 - lon_part),
        (1.0 - lat_part) * lon_part,
        lat_part * lon_part,
    )
    return lax.optimization_barrier(tuple((weight.astype(jnp.bfloat16) for weight in raw_weights)))


def spread_matrix(cell_ids, frac_lat, frac_lon, stride, cells_total):
    is_live = cell_ids >= 0
    corner = jnp.where(is_live, cell_ids, 0)
    weights = bilinear_weights(frac_lat, frac_lon)
    cell_axis = lax.broadcasted_iota(jnp.int32, (1, cells_total), 1)
    matrix = jnp.zeros((cell_ids.shape[0], cells_total), jnp.float32)
    for weight, offset in zip(weights, (0, stride, 1, stride + 1)):
        live_weight = jnp.where(is_live, weight.astype(jnp.float32), 0.0)
        matrix = matrix + jnp.where(
            corner[:, None] + offset == cell_axis, live_weight[:, None], 0.0
        )
    return matrix.astype(jnp.bfloat16)


def forward_piece(spread, col_table, cell_ids, innovation, jacobian):
    interp = jnp.dot(spread, col_table, preferred_element_type=jnp.float32)
    evolved = jnp.sum(interp * jacobian.astype(jnp.float32), axis=1)
    return jnp.where(
        cell_ids >= 0, evolved - innovation.astype(jnp.float32), jnp.zeros((), jnp.float32)
    )


def adjoint_piece(spread, inv_error, departure, jacobian, grad_ext):
    contrib = (
        (inv_error.astype(jnp.float32) * departure)[:, None] * jacobian.astype(jnp.float32)
    ).astype(jnp.bfloat16)
    return grad_ext + lax.dot_general(
        spread, contrib, (((0,), (0,)), ((), ())), preferred_element_type=jnp.float32
    )


def shards(field, obs_jac, obs_frac, obs_innov, obs_rinv, obs_cells):
    lat_rows, lon_cols, width_all = field.shape
    north_row = shifted(field[:1], "lat", -1)
    taller = jnp.concatenate([field, north_row], axis=0)
    east_col = passed_along(taller[:, :1], "lon", -1)
    widened = jnp.concatenate([taller, east_col], axis=1)
    stride = lon_cols + 1
    col_table = widened.reshape(-1, width_all)
    cells_total = col_table.shape[0]
    jac_rows, frac_pair, innov_vals, rinv_vals = (
        lax.all_to_all(obs_jac, ("lat", "lon"), split_axis=0, concat_axis=1, tiled=True),
        lax.all_to_all(obs_frac, ("lat", "lon"), split_axis=0, concat_axis=1, tiled=True),
        lax.all_to_all(obs_innov, ("lat", "lon"), split_axis=0, concat_axis=1, tiled=True),
        lax.all_to_all(obs_rinv, ("lat", "lon"), split_axis=0, concat_axis=1, tiled=True),
    )
    cell_vals = lax.all_to_all(obs_cells, ("lat", "lon"), split_axis=0, concat_axis=1, tiled=True)
    sources = cell_vals.shape[1]
    slots_all = cell_vals.shape[2]
    cells_two = cell_vals.reshape(sources, slots_all)
    frac_three = frac_pair.reshape(sources, 2, slots_all)
    innov_two = innov_vals.reshape(sources, slots_all)
    rinv_two = rinv_vals.reshape(sources, slots_all)
    jac_three = jac_rows.reshape(sources, slots_all, width_all)
    piece = slots_all // 8
    piece_rows = sources * piece

    def take_piece(piece_idx):
        start = piece_idx * piece
        cells_p = lax.dynamic_slice_in_dim(cells_two, start, piece, 1).reshape(-1)
        frac_p = lax.dynamic_slice_in_dim(frac_three, start, piece, 2)
        lat_p = frac_p[:, 0, :].reshape(-1)
        lon_p = frac_p[:, 1, :].reshape(-1)
        innov_p = lax.dynamic_slice_in_dim(innov_two, start, piece, 1).reshape(-1)
        rinv_p = lax.dynamic_slice_in_dim(rinv_two, start, piece, 1).reshape(-1)
        jac_p = lax.dynamic_slice_in_dim(jac_three, start, piece, 1).reshape(piece_rows, width_all)
        return (cells_p, lat_p, lon_p, innov_p, rinv_p, jac_p)

    def store_piece(departs, departure, piece_idx):
        return lax.dynamic_update_slice_in_dim(
            departs, departure.reshape(sources, piece), piece_idx * piece, 1
        )

    def full_turn(piece_idx, state_pair):
        grad_ext, departs = state_pair
        cells_p, lat_p, lon_p, innov_p, rinv_p, jac_p = take_piece(piece_idx)
        spread = spread_matrix(cells_p, lat_p, lon_p, stride, cells_total)
        departure = forward_piece(spread, col_table, cells_p, innov_p, jac_p)
        grad_ext = adjoint_piece(spread, rinv_p, departure, jac_p, grad_ext)
        return (grad_ext, store_piece(departs, departure, piece_idx))

    grad_start = jnp.zeros((cells_total, width_all), jnp.float32)
    depart_start = jnp.zeros((sources, slots_all), jnp.float32)
    live_most = jnp.max(jnp.sum((cells_two >= 0).astype(jnp.int32), axis=1))
    pieces_used = (live_most + piece - 1) // piece
    grad_ext, departs = lax.fori_loop(0, pieces_used, full_turn, (grad_start, depart_start))
    grad_grid = grad_ext.reshape(lat_rows + 1, stride, width_all)
    east_back = passed_along(grad_grid[:, lon_cols:], "lon", 1)
    grad_grid = grad_grid[:, :lon_cols].at[:, :1].add(east_back)
    north_back = shifted(grad_grid[lat_rows:], "lat", 1)
    field_grad = grad_grid[:lat_rows].at[:1].add(north_back)
    departures = lax.all_to_all(
        departs.reshape(1, sources, slots_all),
        ("lat", "lon"),
        split_axis=1,
        concat_axis=0,
        tiled=True,
    )
    return (departures, field_grad)


def solution(mesh):
    placed = (
        P("lat", "lon", None),
        P(None, ("lat", "lon"), None, None),
        P(None, ("lat", "lon"), None, None),
        P(None, ("lat", "lon"), None),
        P(None, ("lat", "lon"), None),
        P(None, ("lat", "lon"), None),
    )
    return jax.shard_map(
        shards,
        mesh=mesh,
        in_specs=placed,
        out_specs=(P(None, ("lat", "lon"), None), P("lat", "lon", None)),
        check_vma=False,
    )
```

profile of v0, /device:TPU:0, one launch (start us, length us, event | category | flops | bytes accessed | tf_op | source)
XLA Modules:
  0.0 184.6 jit_solution(12065559047575675687)
XLA Ops:
  0.6 1.3 copy.22
  1.9 7.3 %all-to-all-start.4 = ((bf16[32,1,128]{2,1,0:T(2,128)(2,1)}), bf16[32,1,128]{2,1,0:T(2,128)(2,1)S(1)}, u32[]{:S(2)}, u32[]{:S(2)}) async-start(bf16[32,1,128]{2,1,0:T(2,128)(2,1)} %copy.22), calls=%async_computation.4 | async-start | bytes 32768 | tf_op jit(solution)/shard_map/all_to_all | solution.py:74
  10.0 6.4 %all-to-all-done.4 = bf16[32,1,128]{2,1,0:T(2,128)(2,1)S(1)} async-done(((bf16[32,1,128]{2,1,0:T(2,128)(2,1)}), bf16[32,1,128]{2,1,0:T(2,128)(2,1)S(1)}, u32[]{:S(2)}, u32[]{:S(2)}) %all-to-all-start.4) | async-done | bytes 8224 | tf_op jit(solution)/shard_map/all_to_all | solution.py:74
  16.3 8.8 %all_to_all.27 = bf16[32,1,128]{2,1,0:T(2,128)(2,1)S(1)} all-to-all(bf16[32,1,128]{2,1,0:T(2,128)(2,1)S(1)} %copy.21), channel_id=1, replica_groups=mesh['lat'=4,'lon'=8] {'lat','lon'}, dimensions={0} | all-to-all | bytes 16384 | tf_op jit(solution)/shard_map/all_to_all | solution.py:75
  25.2 9.6 %all_to_all.28 = s32[32,1,128]{2,1,0:T(1,128)S(1)} all-to-all(s32[32,1,128]{2,1,0:T(1,128)} %param.17), channel_id=1, replica_groups=mesh['lat'=4,'lon'=8] {'lat','lon'}, dimensions={0} | all-to-all | bytes 32768 | tf_op jit(solution)/shard_map/all_to_all | solution.py:77
  34.8 9.6 %all_to_all.29 = bf16[32,1,2,128]{3,2,1,0:T(2,128)(2,1)S(1)} all-to-all(bf16[32,1,2,128]{3,2,1,0:T(2,128)(2,1)} %param.14), channel_id=1, replica_groups=mesh['lat'=4,'lon'=8] {'lat','lon'}, dimensions={0} | all-to-all | bytes 32768 | tf_op jit(solution)/shard_map/all_to_all | solution.py:73
  44.4 3.7 %all-to-all-start.3 = ((bf16[32,1,128,384]{3,2,1,0:T(8,128)(2,1)}), bf16[32,1,128,384]{3,2,1,0:T(8,128)(2,1)}, u32[]{:S(2)}, u32[]{:S(2)}) async-start(bf16[32,1,128,384]{3,2,1,0:T(8,128)(2,1)} %param.13), calls=%async_computation.3 | async-start | bytes 6291456 | tf_op jit(solution)/shard_map/all_to_all | solution.py:72
  48.1 1.3 collective-permute-start
  49.4 1.7 collective-permute-done
  51.2 4.5 %collective-permute-start.1 = (bf16[17,1,384]{2,1,0:T(2,128)(2,1)S(1)}, bf16[17,1,384]{2,1,0:T(2,128)(2,1)S(1)}, u32[]{:S(2)}, u32[]{:S(2)}) collective-permute-start(bf16[17,1,384]{2,1,0:T(2,128)(2,1)S(1)} %slice.82), channel_id=1, source_target_pairs={{0,7},{1,0},{2,1},{3,2},{4,3},{5,4},{6,5},{7,6},{8,15},{9,8},{10,9... | collective-permute-start | bytes 39176 | tf_op jit(solution)/shard_map/ppermute | solution.py:16
  55.7 44.9 %collective-permute-done.1 = bf16[17,1,384]{2,1,0:T(2,128)(2,1)S(1)} collective-permute-done((bf16[17,1,384]{2,1,0:T(2,128)(2,1)S(1)}, bf16[17,1,384]{2,1,0:T(2,128)(2,1)S(1)}, u32[]{:S(2)}, u32[]{:S(2)}) %collective-permute-start.1) | collective-permute-done | bytes 13088 | tf_op jit(solution)/shard_map/ppermute | solution.py:16
  102.2 18.4 %all-to-all-done.3 = bf16[32,1,128,384]{3,2,1,0:T(8,128)(2,1)} async-done(((bf16[32,1,128,384]{3,2,1,0:T(8,128)(2,1)}), bf16[32,1,128,384]{3,2,1,0:T(8,128)(2,1)}, u32[]{:S(2)}, u32[]{:S(2)}) %all-to-all-start.3) | async-done | bytes 3145760 | tf_op jit(solution)/shard_map/all_to_all | solution.py:72
  121.2 12.5 %while.14 = (s32[]{:T(128)}, f32[289,384]{1,0:T(8,128)S(1)}, f32[32,128]{1,0:T(8,128)}, s32[]{:T(128)}, s32[32,128]{1,0:T(8,128)S(1)}, /*index=5*/bf16[32,2,128]...) while((s32[]{:T(128)}, f32[289,384]{1,0:T(8,128)S(1)}, ...), condition=%wide.region_4.5_spmd, body=%wide.region_2.4_spmd.sunk | while | flops 231940992 | bytes 6360035 | solution.py:116
  121.7 1.1 constant_dynamic-slice_fusion.7
  123.2 1.4 fusion.9
  124.8 1.1 convolution_add_fusion.2
  126.1 1.3 dynamic_update_slice.4
  129.4 1.4 fusion.9
  131.1 1.1 convolution_add_fusion.2
  132.3 1.4 dynamic_update_slice.4
  133.8 37.5 %collective-permute-start.2 = (f32[17,1,384]{2,1,0:T(1,128)S(1)}, f32[17,1,384]{2,1,0:T(1,128)S(1)}, u32[]{:S(2)}, u32[]{:S(2)}) collective-permute-start(f32[17,1,384]{2,1,0:T(1,128)S(1)} %slice.85), channel_id=1, source_target_pairs={{0,1},{1,2},{2,3},{3,4},{4,5},{5,6},{6,7},{7,0},{8,9},{9,10},{10,1... | collective-permute-start | bytes 78344 | tf_op jit(solution)/shard_map/ppermute | solution.py:16
  171.4 5.3 %all-to-all-start.5 = ((f32[1,32,128]{2,0,1:T(1,128)}), f32[1,32,128]{2,0,1:T(1,128)S(1)}, u32[]{:S(2)}, u32[]{:S(2)}) async-start(f32[1,32,128]{2,0,1:T(1,128)} %bitcast.4), calls=%async_computation.5 | async-start | bytes 32768 | tf_op jit(solution)/shard_map/all_to_all | solution.py:122
  176.9 2.2 %collective-permute-start.3 = (f32[1,16,384]{2,1,0:T(8,128)S(1)}, f32[1,16,384]{2,1,0:T(8,128)S(1)}, u32[]{:S(2)}, u32[]{:S(2)}) collective-permute-start(f32[1,16,384]{2,1,0:T(8,128)S(1)} %slice.88), channel_id=1, source_target_pairs={{0,8},{8,16},{16,24},{1,9},{9,17},{17,25},{2,10},{10,18},{18,26},{... | collective-permute-start | bytes 73736 | tf_op jit(solution)/shard_map/ppermute | solution.py:10
  179.1 4.7 %all-to-all-done.5 = f32[1,32,128]{2,0,1:T(1,128)S(1)} async-done(((f32[1,32,128]{2,0,1:T(1,128)}), f32[1,32,128]{2,0,1:T(1,128)S(1)}, u32[]{:S(2)}, u32[]{:S(2)}) %all-to-all-start.5) | async-done | bytes 16416 | tf_op jit(solution)/shard_map/all_to_all | solution.py:122
  (67 shorter events, 6.8 us)
Async XLA Ops:
  1.9 14.4 %all-to-all-start.4 = ((bf16[32,1,128]{2,1,0:T(2,128)(2,1)}), bf16[32,1,128]{2,1,0:T(2,128)(2,1)S(1)}, u32[]{:S(2)}, u32[]{:S(2)}) async-start(bf16[32,1,128]{2,1,0:T(2,128)(2,1)} %copy.22), calls=%async_computation.4 | async-start | bytes 32768 | tf_op jit(solution)/shard_map/all_to_all | solution.py:74
  44.4 3.7 %copy-start.1 = (bf16[16,16,384]{2,1,0:T(8,128)(2,1)S(1)}, bf16[16,16,384]{2,1,0:T(8,128)(2,1)}, u32[]{:S(2)}) copy-start(bf16[16,16,384]{2,1,0:T(8,128)(2,1)} %param.12) | copy-start | bytes 589828
  44.4 76.2 %all-to-all-start.3 = ((bf16[32,1,128,384]{3,2,1,0:T(8,128)(2,1)}), bf16[32,1,128,384]{3,2,1,0:T(8,128)(2,1)}, u32[]{:S(2)}, u32[]{:S(2)}) async-start(bf16[32,1,128,384]{3,2,1,0:T(8,128)(2,1)} %param.13), calls=%async_computation.3 | async-start | bytes 6291456 | tf_op jit(solution)/shard_map/all_to_all | solution.py:72
  48.1 3.1 %collective-permute-start = (bf16[1,16,384]{2,1,0:T(8,128)(2,1)S(1)}, bf16[1,16,384]{2,1,0:T(8,128)(2,1)S(1)}, u32[]{:S(2)}, u32[]{:S(2)}) collective-permute-start(bf16[1,16,384]{2,1,0:T(8,128)(2,1)S(1)} %slice.74), channel_id=1, source_target_pairs={{8,0},{16,8},{24,16},{9,1},{17,9},{25,17},{10,2},{18,10},{26,18},{... | collective-permute-start | bytes 36872 | tf_op jit(solution)/shard_map/ppermute | solution.py:10
  51.2 49.5 %collective-permute-start.1 = (bf16[17,1,384]{2,1,0:T(2,128)(2,1)S(1)}, bf16[17,1,384]{2,1,0:T(2,128)(2,1)S(1)}, u32[]{:S(2)}, u32[]{:S(2)}) collective-permute-start(bf16[17,1,384]{2,1,0:T(2,128)(2,1)S(1)} %slice.82), channel_id=1, source_target_pairs={{0,7},{1,0},{2,1},{3,2},{4,3},{5,4},{6,5},{7,6},{8,15},{9,8},{10,9... | collective-permute-start | bytes 39176 | tf_op jit(solution)/shard_map/ppermute | solution.py:16
  133.8 42.9 %collective-permute-start.2 = (f32[17,1,384]{2,1,0:T(1,128)S(1)}, f32[17,1,384]{2,1,0:T(1,128)S(1)}, u32[]{:S(2)}, u32[]{:S(2)}) collective-permute-start(f32[17,1,384]{2,1,0:T(1,128)S(1)} %slice.85), channel_id=1, source_target_pairs={{0,1},{1,2},{2,3},{3,4},{4,5},{5,6},{6,7},{7,0},{8,9},{9,10},{10,1... | collective-permute-start | bytes 78344 | tf_op jit(solution)/shard_map/ppermute | solution.py:16
  171.4 12.4 %all-to-all-start.5 = ((f32[1,32,128]{2,0,1:T(1,128)}), f32[1,32,128]{2,0,1:T(1,128)S(1)}, u32[]{:S(2)}, u32[]{:S(2)}) async-start(f32[1,32,128]{2,0,1:T(1,128)} %bitcast.4), calls=%async_computation.5 | async-start | bytes 32768 | tf_op jit(solution)/shard_map/all_to_all | solution.py:122
  176.9 6.9 %collective-permute-start.3 = (f32[1,16,384]{2,1,0:T(8,128)S(1)}, f32[1,16,384]{2,1,0:T(8,128)S(1)}, u32[]{:S(2)}, u32[]{:S(2)}) collective-permute-start(f32[1,16,384]{2,1,0:T(8,128)S(1)} %slice.88), channel_id=1, source_target_pairs={{0,8},{8,16},{16,24},{1,9},{9,17},{17,25},{2,10},{10,18},{18,26},{... | collective-permute-start | bytes 73736 | tf_op jit(solution)/shard_map/ppermute | solution.py:10
  183.8 0.8 copy-start
where the time goes:
time: 186 us; the launch traced here: 185 us
  waiting for transfers between devices  76.1 us (41%)
  starting transfers between devices  61.8 us (33%)
  blocking collectives  28 us (15%)
  local copies, waits for them, and re-layouts  10.5 us (6%)
  matrix products  5.04 us (3%)
    ppermute x2, waiting for transfers between devices, passed_along(): return lax.ppermute(value, axis, pairs)  44.9 us
    ppermute x2, starting transfers between devices, passed_along(): return lax.ppermute(value, axis, pairs)  42.1 us
    all_to_all x1, waiting for transfers between devices, shards(): lax.all_to_all(obs_jac, ('lat', 'lon'), split_axis=0, concat_axis=1, tile...  18.4 us
    all_to_all x1, blocking collectives, shards(): lax.all_to_all(obs_cells, ('lat', 'lon'), split_axis=0, concat_axis=1, ti...  9.61 us
    all_to_all x1, blocking collectives, shards(): lax.all_to_all(obs_frac, ('lat', 'lon'), split_axis=0, concat_axis=1, til...  9.61 us
    all_to_all x1, blocking collectives, shards(): lax.all_to_all(obs_rinv, ('lat', 'lon'), split_axis=0, concat_axis=1, til...  8.82 us
    all_to_all x1, starting transfers between devices, shards(): lax.all_to_all(obs_innov, ('lat', 'lon'), split_axis=0, concat_axis=1, ti...  7.33 us
    all_to_all x1, waiting for transfers between devices, shards(): lax.all_to_all(obs_innov, ('lat', 'lon'), split_axis=0, concat_axis=1, ti...  6.35 us
  transfers between devices with their start and end apart: 7, of which 5 were waited for; matrix products, arithmetic and copies ran while one was open for 1% of the time, Pallas kernels for 0%

commit v1 on v0

--- a/solution.py
+++ b/solution.py
@@ -71,7 +71,15 @@
     jac_rows, frac_pair, innov_vals, rinv_vals = (
         lax.all_to_all(obs_jac, ("lat", "lon"), split_axis=0, concat_axis=1, tiled=True),
         lax.all_to_all(obs_frac, ("lat", "lon"), split_axis=0, concat_axis=1, tiled=True),
-        lax.all_to_all(obs_innov, ("lat", "lon"), split_axis=0, concat_axis=1, tiled=True),
+        jnp.concatenate(
+            lax.all_to_all(
+                jnp.stack(jnp.split(obs_innov, lax.axis_size(("lat", "lon")), axis=0)),
+                ("lat", "lon"),
+                0,
+                0,
+            ),
+            axis=1,
+        ),
         lax.all_to_all(obs_rinv, ("lat", "lon"), split_axis=0, concat_axis=1, tiled=True),
     )
     cell_vals = lax.all_to_all(obs_cells, ("lat", "lon"), split_axis=0, concat_axis=1, tiled=True)

time: 186 us -> 224 us (1.20)
  local copies, waits for them, and re-layouts: 10.5 us -> 47.4 us
    unnamed x10 -> x40, local copies, waits for them, and re-layouts: 2.81 us -> 38.5 us
where the time goes in v1:
time: 224 us; the launch traced here: 221 us
  waiting for transfers between devices  76.1 us (34%)
  starting transfers between devices  61.8 us (28%)
  local copies, waits for them, and re-layouts  47.4 us (21%)
  blocking collectives  28 us (12%)
  matrix products  5.04 us (2%)
    ppermute x2, waiting for transfers between devices, passed_along(): return lax.ppermute(value, axis, pairs)  44.9 us
    ppermute x2, starting transfers between devices, passed_along(): return lax.ppermute(value, axis, pairs)  42.1 us
    unnamed x40, local copies, waits for them, and re-layouts  38.5 us
    all_to_all x1, waiting for transfers between devices, shards(): lax.all_to_all(obs_jac, ('lat', 'lon'), split_axis=0, concat_axis=1, tile...  18.4 us
    all_to_all x1, blocking collectives, shards(): lax.all_to_all(obs_cells, ('lat', 'lon'), split_axis=0, concat_axis=1, ti...  9.61 us
    all_to_all x1, blocking collectives, shards(): lax.all_to_all(obs_frac, ('lat', 'lon'), split_axis=0, concat_axis=1, til...  9.61 us
    all_to_all x1, blocking collectives, shards(): lax.all_to_all(obs_rinv, ('lat', 'lon'), split_axis=0, concat_axis=1, til...  8.82 us
    all_to_all x1, starting transfers between devices, shards(): lax.all_to_all(jnp.stack(jnp.split(obs_innov, lax.axis_size(('lat', 'lon'...  7.33 us
  transfers between devices with their start and end apart: 7, of which 5 were waited for; matrix products, arithmetic and copies ran while one was open for 1% of the time, Pallas kernels for 0%

profile of v1, /device:TPU:0, one launch (start us, length us, event | category | flops | bytes accessed | tf_op | source)
XLA Modules:
  0.0 221.5 jit_solution(17571124371428709415)
XLA Ops:
  1.8 1.2 constant_dynamic-update-slice_fusion.32
  5.4 1.2 constant_dynamic-update-slice_fusion.29
  7.8 1.2 constant_dynamic-update-slice_fusion.27
  18.6 1.2 constant_dynamic-update-slice_fusion.18
  38.9 7.3 %all-to-all-start.4 = ((bf16[32,1,1,128]{3,2,1,0:T(2,128)(2,1)}), bf16[32,1,1,128]{3,2,1,0:T(2,128)(2,1)S(1)}, u32[]{:S(2)}, u32[]{:S(2)}) async-start(bf16[32,1,1,128]{3,2,1,0:T(2,128)(2,1)} %constant_dynamic-update-slice_fusion.2), calls=%async_computation.4 | async-start | bytes 32768 | tf_op jit(solution)/shard_map/all_to_all | solution.py:75
  46.9 6.4 %all-to-all-done.4 = bf16[32,1,1,128]{3,2,1,0:T(2,128)(2,1)S(1)} async-done(((bf16[32,1,1,128]{3,2,1,0:T(2,128)(2,1)}), bf16[32,1,1,128]{3,2,1,0:T(2,128)(2,1)S(1)}, u32[]{:S(2)}, u32[]{:S(2)}) %all-to-all-start.4) | async-done | bytes 8224 | tf_op jit(solution)/shard_map/all_to_all | solution.py:75
  53.3 8.8 %all_to_all.53 = bf16[32,1,128]{2,1,0:T(2,128)(2,1)S(1)} all-to-all(bf16[32,1,128]{2,1,0:T(2,128)(2,1)S(1)} %copy.20), channel_id=1, replica_groups=mesh['lat'=4,'lon'=8] {'lat','lon'}, dimensions={0} | all-to-all | bytes 16384 | tf_op jit(solution)/shard_map/all_to_all | solution.py:83
  62.1 9.6 %all_to_all.54 = s32[32,1,128]{2,1,0:T(1,128)S(1)} all-to-all(s32[32,1,128]{2,1,0:T(1,128)} %param.17), channel_id=1, replica_groups=mesh['lat'=4,'lon'=8] {'lat','lon'}, dimensions={0} | all-to-all | bytes 32768 | tf_op jit(solution)/shard_map/all_to_all | solution.py:85
  71.7 9.6 %all_to_all.55 = bf16[32,1,2,128]{3,2,1,0:T(2,128)(2,1)S(1)} all-to-all(bf16[32,1,2,128]{3,2,1,0:T(2,128)(2,1)} %param.14), channel_id=1, replica_groups=mesh['lat'=4,'lon'=8] {'lat','lon'}, dimensions={0} | all-to-all | bytes 32768 | tf_op jit(solution)/shard_map/all_to_all | solution.py:73
  81.3 3.7 %all-to-all-start.3 = ((bf16[32,1,128,384]{3,2,1,0:T(8,128)(2,1)}), bf16[32,1,128,384]{3,2,1,0:T(8,128)(2,1)}, u32[]{:S(2)}, u32[]{:S(2)}) async-start(bf16[32,1,128,384]{3,2,1,0:T(8,128)(2,1)} %param.13), calls=%async_computation.3 | async-start | bytes 6291456 | tf_op jit(solution)/shard_map/all_to_all | solution.py:72
  85.0 1.3 collective-permute-start
  86.3 1.7 collective-permute-done
  88.1 4.5 %collective-permute-start.1 = (bf16[17,1,384]{2,1,0:T(2,128)(2,1)S(1)}, bf16[17,1,384]{2,1,0:T(2,128)(2,1)S(1)}, u32[]{:S(2)}, u32[]{:S(2)}) collective-permute-start(bf16[17,1,384]{2,1,0:T(2,128)(2,1)S(1)} %slice.82), channel_id=1, source_target_pairs={{0,7},{1,0},{2,1},{3,2},{4,3},{5,4},{6,5},{7,6},{8,15},{9,8},{10,9... | collective-permute-start | bytes 39176 | tf_op jit(solution)/shard_map/ppermute | solution.py:16
  92.7 44.9 %collective-permute-done.1 = bf16[17,1,384]{2,1,0:T(2,128)(2,1)S(1)} collective-permute-done((bf16[17,1,384]{2,1,0:T(2,128)(2,1)S(1)}, bf16[17,1,384]{2,1,0:T(2,128)(2,1)S(1)}, u32[]{:S(2)}, u32[]{:S(2)}) %collective-permute-start.1) | collective-permute-done | bytes 13088 | tf_op jit(solution)/shard_map/ppermute | solution.py:16
  139.2 18.4 %all-to-all-done.3 = bf16[32,1,128,384]{3,2,1,0:T(8,128)(2,1)} async-done(((bf16[32,1,128,384]{3,2,1,0:T(8,128)(2,1)}), bf16[32,1,128,384]{3,2,1,0:T(8,128)(2,1)}, u32[]{:S(2)}, u32[]{:S(2)}) %all-to-all-start.3) | async-done | bytes 3145760 | tf_op jit(solution)/shard_map/all_to_all | solution.py:72
  158.2 12.5 %while.14 = (s32[]{:T(128)}, f32[289,384]{1,0:T(8,128)S(1)}, f32[32,128]{1,0:T(8,128)}, s32[]{:T(128)}, s32[32,128]{1,0:T(8,128)S(1)}, /*index=5*/bf16[32,2,128]...) while((s32[]{:T(128)}, f32[289,384]{1,0:T(8,128)S(1)}, ...), condition=%wide.region_4.5_spmd, body=%wide.region_2.4_spmd.sunk | while | flops 231940992 | bytes 6360035 | solution.py:124
  160.1 1.4 fusion.9
  163.0 1.3 dynamic_update_slice.4
  166.3 1.4 fusion.9
  169.3 1.4 dynamic_update_slice.4
  170.8 37.5 %collective-permute-start.2 = (f32[17,1,384]{2,1,0:T(1,128)S(1)}, f32[17,1,384]{2,1,0:T(1,128)S(1)}, u32[]{:S(2)}, u32[]{:S(2)}) collective-permute-start(f32[17,1,384]{2,1,0:T(1,128)S(1)} %slice.85), channel_id=1, source_target_pairs={{0,1},{1,2},{2,3},{3,4},{4,5},{5,6},{6,7},{7,0},{8,9},{9,10},{10,1... | collective-permute-start | bytes 78344 | tf_op jit(solution)/shard_map/ppermute | solution.py:16
  208.3 5.3 %all-to-all-start.5 = ((f32[1,32,128]{2,0,1:T(1,128)}), f32[1,32,128]{2,0,1:T(1,128)S(1)}, u32[]{:S(2)}, u32[]{:S(2)}) async-start(f32[1,32,128]{2,0,1:T(1,128)} %bitcast.36), calls=%async_computation.5 | async-start | bytes 32768 | tf_op jit(solution)/shard_map/all_to_all | solution.py:130
  213.8 2.2 collective-permute-start.3
  216.0 4.7 %all-to-all-done.5 = f32[1,32,128]{2,0,1:T(1,128)S(1)} async-done(((f32[1,32,128]{2,0,1:T(1,128)}), f32[1,32,128]{2,0,1:T(1,128)S(1)}, u32[]{:S(2)}, u32[]{:S(2)}) %all-to-all-start.5) | async-done | bytes 16416 | tf_op jit(solution)/shard_map/all_to_all | solution.py:130
  (98 shorter events, 43.5 us)
Async XLA Ops:
  38.9 14.4 %all-to-all-start.4 = ((bf16[32,1,1,128]{3,2,1,0:T(2,128)(2,1)}), bf16[32,1,1,128]{3,2,1,0:T(2,128)(2,1)S(1)}, u32[]{:S(2)}, u32[]{:S(2)}) async-start(bf16[32,1,1,128]{3,2,1,0:T(2,128)(2,1)} %constant_dynamic-update-slice_fusion.2), calls=%async_computation.4 | async-start | bytes 32768 | tf_op jit(solution)/shard_map/all_to_all | solution.py:75
  81.3 3.7 %copy-start.1 = (bf16[16,16,384]{2,1,0:T(8,128)(2,1)S(1)}, bf16[16,16,384]{2,1,0:T(8,128)(2,1)}, u32[]{:S(2)}) copy-start(bf16[16,16,384]{2,1,0:T(8,128)(2,1)} %param.12) | copy-start | bytes 589828
  81.3 76.2 %all-to-all-start.3 = ((bf16[32,1,128,384]{3,2,1,0:T(8,128)(2,1)}), bf16[32,1,128,384]{3,2,1,0:T(8,128)(2,1)}, u32[]{:S(2)}, u32[]{:S(2)}) async-start(bf16[32,1,128,384]{3,2,1,0:T(8,128)(2,1)} %param.13), calls=%async_computation.3 | async-start | bytes 6291456 | tf_op jit(solution)/shard_map/all_to_all | solution.py:72
  85.0 3.1 %collective-permute-start = (bf16[1,16,384]{2,1,0:T(8,128)(2,1)S(1)}, bf16[1,16,384]{2,1,0:T(8,128)(2,1)S(1)}, u32[]{:S(2)}, u32[]{:S(2)}) collective-permute-start(bf16[1,16,384]{2,1,0:T(8,128)(2,1)S(1)} %slice.74), channel_id=1, source_target_pairs={{8,0},{16,8},{24,16},{9,1},{17,9},{25,17},{10,2},{18,10},{26,18},{... | collective-permute-start | bytes 36872 | tf_op jit(solution)/shard_map/ppermute | solution.py:10
  88.1 49.5 %collective-permute-start.1 = (bf16[17,1,384]{2,1,0:T(2,128)(2,1)S(1)}, bf16[17,1,384]{2,1,0:T(2,128)(2,1)S(1)}, u32[]{:S(2)}, u32[]{:S(2)}) collective-permute-start(bf16[17,1,384]{2,1,0:T(2,128)(2,1)S(1)} %slice.82), channel_id=1, source_target_pairs={{0,7},{1,0},{2,1},{3,2},{4,3},{5,4},{6,5},{7,6},{8,15},{9,8},{10,9... | collective-permute-start | bytes 39176 | tf_op jit(solution)/shard_map/ppermute | solution.py:16
  170.8 42.9 %collective-permute-start.2 = (f32[17,1,384]{2,1,0:T(1,128)S(1)}, f32[17,1,384]{2,1,0:T(1,128)S(1)}, u32[]{:S(2)}, u32[]{:S(2)}) collective-permute-start(f32[17,1,384]{2,1,0:T(1,128)S(1)} %slice.85), channel_id=1, source_target_pairs={{0,1},{1,2},{2,3},{3,4},{4,5},{5,6},{6,7},{7,0},{8,9},{9,10},{10,1... | collective-permute-start | bytes 78344 | tf_op jit(solution)/shard_map/ppermute | solution.py:16
  208.3 12.4 %all-to-all-start.5 = ((f32[1,32,128]{2,0,1:T(1,128)}), f32[1,32,128]{2,0,1:T(1,128)S(1)}, u32[]{:S(2)}, u32[]{:S(2)}) async-start(f32[1,32,128]{2,0,1:T(1,128)} %bitcast.36), calls=%async_computation.5 | async-start | bytes 32768 | tf_op jit(solution)/shard_map/all_to_all | solution.py:130
  213.8 6.9 %collective-permute-start.3 = (f32[1,16,384]{2,1,0:T(8,128)S(1)}, f32[1,16,384]{2,1,0:T(8,128)S(1)}, u32[]{:S(2)}, u32[]{:S(2)}) collective-permute-start(f32[1,16,384]{2,1,0:T(8,128)S(1)} %slice.88), channel_id=1, source_target_pairs={{0,8},{8,16},{16,24},{1,9},{9,17},{17,25},{2,10},{10,18},{18,26},{... | collective-permute-start | bytes 73736 | tf_op jit(solution)/shard_map/ppermute | solution.py:10
  220.7 0.8 copy-start
